TPU v7x, 256 devices: a whole 4x4x8 slice. The times are simulated.
256 devices in a mesh: lat: 16 (over y_hi, z), orient: 16 (over y_lo, x, core).
Axes of the slice: x: 4, y: 4 (y_hi: 2, y_lo: 2; y = y_hi * 2 + y_lo), z: 8, core: 2. Of those that a mesh axis runs over, the one named last changes fastest.
Arguments:
- features: bfloat16 [16, 32, 64, 8192], P('orient', None, 'lat'), may hold values from -6 to 6
- mix_weights: bfloat16 [2, 3, 32, 32], replicated, may hold values from -0.625 to 0.625
- kernels: bfloat16 [2, 9, 32, 32], replicated, may hold values from -0.375 to 0.375
- bias_terms: float32 [2, 32], replicated, may hold values from -3 to 3
Outputs:
- responses: bfloat16 [16, 32, 64, 8192], P('orient', None, 'lat')
All inputs are finite; a program needn't handle non-finite values.
Results may differ from a plain program's by a relative error of at most 0.0061.
Values may be sent and summed in bfloat16 or wider, within the bound.
A program may use at most 128 MiB of HBM per device.

v0:
```python
import jax
import jax.numpy as jnp
import numpy as np
from jax import lax
from jax.sharding import PartitionSpec as P

LAYERS = 2


CYCLE_PLACE = np.array([0, 1, 2, 7, -1, 3, 6, 5, 4])
CYCLE_PAIRS = np.outer((CYCLE_PLACE >= 0).astype(np.float32), (CYCLE_PLACE >= 0).astype(np.float32))
CENTER_ONE = np.outer((CYCLE_PLACE < 0).astype(np.float32), (CYCLE_PLACE < 0).astype(np.float32))


def extended_2(block, sides, width, periodic):
    for axis, dim in sides:
        count = lax.axis_size(axis)
        forward = [(i, i + 1) for i in range(count - 1)]
        if periodic:
            forward.append((count - 1, 0))
        backward = [(target, source) for source, target in forward]
        low = lax.ppermute(
            lax.slice_in_dim(block, block.shape[dim] - width, None, axis=dim), axis, forward
        )
        high = lax.ppermute(lax.slice_in_dim(block, 0, width, axis=dim), axis, backward)
        block = jnp.concatenate([low, block, high], axis=dim)
    return block


def rotation_table(orient):
    half_turn = orient.astype(jnp.float32) * 0.5
    positions = jnp.asarray(CYCLE_PLACE).astype(jnp.float32)
    distance = jnp.mod(positions[:, None] - positions[None, :] - half_turn + 4.0, 8.0) - 4.0
    weight = jnp.maximum(0.0, 1.0 - jnp.abs(distance))
    return weight * jnp.asarray(CYCLE_PAIRS).astype(jnp.float32) + jnp.asarray(CENTER_ONE).astype(
        jnp.float32
    )


def rotated_kernels(kernel, orient):
    table = rotation_table(orient)
    return jnp.einsum(
        "ab,bij->aij", table, kernel.astype(jnp.float32), precision=lax.Precision.HIGHEST
    ).astype(jnp.bfloat16)


def mix_orients(extended, mixing, count):
    running = None
    for offset in range(3):
        term = jnp.einsum(
            "ij,ojrw->oirw",
            mixing[offset],
            extended[offset : offset + count],
            preferred_element_type=jnp.float32,
        )
        running = term if running is None else running + term
    return running.astype(jnp.bfloat16)


def conv_layer(padded, rotated, bias_row, out_rows):
    row_stack = jnp.stack(
        [padded[:, :, row_start : row_start + out_rows, :] for row_start in range(3)], axis=1
    )
    running = None
    for col_index in range(3):
        col_shift = col_index - 1
        taps = rotated[:, col_index::3]
        term = jnp.einsum("otij,otjrw->oirw", taps, row_stack, preferred_element_type=jnp.float32)
        term = jnp.roll(term, -col_shift, axis=3)
        running = term if running is None else running + term
    return jax.nn.relu(running + bias_row[None, :, None, None]).astype(jnp.bfloat16)


def local(features, mix_weights, kernels, bias_terms):
    count = features.shape[0]
    rows = features.shape[2]
    orients_here = lax.axis_index("orient") * count + jnp.arange(count, dtype=jnp.int32)
    rotations = [
        jax.vmap(lambda orient, kernel=kernels[layer_index]: rotated_kernels(kernel, orient))(
            orients_here
        )
        for layer_index in range(LAYERS)
    ]
    current = features
    for layer_index in range(LAYERS):
        extended = extended_2(current, (("orient", 0),), 1, True)
        mixed_feats = mix_orients(extended, mix_weights[layer_index], count)
        padded = extended_2(mixed_feats, (("lat", 2),), 1, False)
        current = conv_layer(padded, rotations[layer_index], bias_terms[layer_index], rows)
    return current


def solution(mesh):
    in_specs = (P("orient", None, "lat", None), P(), P(), P())
    out_specs = P("orient", None, "lat", None)
    return jax.shard_map(local, mesh=mesh, in_specs=in_specs, out_specs=out_specs, check_vma=False)
```

profile of v0, /device:TPU:16, one launch (start us, length us, event | category | flops | bytes accessed | tf_op | source)
XLA Modules:
  0.0 125.0 jit_solution(11293438762375746691)
XLA Ops:
  0.0 0.0 copy-start
  0.0 4.2 %copy.32 = bf16[1,32,4,8192]{3,1,2,0:T(8,128)(2,1)} copy(bf16[1,32,4,8192]{3,2,1,0:T(4,128)(2,1)} %param.7) | data formatting | bytes 4194304 | tf_op args[0]
  4.2 2.9 %collective-permute-start.1 = (bf16[1,32,4,8192]{3,1,2,0:T(8,128)(2,1)}, bf16[1,32,4,8192]{3,1,2,0:T(8,128)(2,1)}, u32[]{:S(2)}, u32[]{:S(2)}) collective-permute-start(bf16[1,32,4,8192]{3,1,2,0:T(8,128)(2,1)} %copy.32), channel_id=1, source_target_pairs={{1,0},{2,1},{3,2},{4,3},{5,4},{6,5},{7,6},{8,7},{9,8},{10,9},{11,1... | collective-permute-start | bytes 6291464 | tf_op jit(solution)/shard_map/ppermute | solution.py:25
  7.1 0.0 collective-permute-start
  7.1 0.0 copy-done
  7.1 0.0 copy-done.3
  7.1 3.0 %fusion.25 = f32[4,8192,32]{1,2,0:T(8,128)S(1)} fusion(bf16[32,4,8192]{2,1,0:T(4,128)(2,1)S(1)} %bitcast.211, bf16[2,3,32,32]{3,2,1,0:T(8,128)(2,1)S(1)} %copy-done.3), kind=kOutput, calls=%fused_computation.43 | convolution fusion | flops 67108864 | bytes 6299648 | tf_op jit(solution)/shard_map/ij,ojrw->oirw/dot_general | solution.py:50
  10.1 20.9 %collective-permute-done.1 = bf16[1,32,4,8192]{3,1,2,0:T(8,128)(2,1)} collective-permute-done((bf16[1,32,4,8192]{3,1,2,0:T(8,128)(2,1)}, bf16[1,32,4,8192]{3,1,2,0:T(8,128)(2,1)}, u32[]{:S(2)}, u32[]{:S(2)}) %collective-permute-start.1) | collective-permute-done | bytes 2097184 | tf_op jit(solution)/shard_map/ppermute | solution.py:25
  31.0 2.3 %fusion.22 = f32[4,8192,32]{1,2,0:T(8,128)S(1)} fusion(bf16[1,32,4,8192]{3,1,2,0:T(8,128)(2,1)} %collective-permute-done.1, bf16[2,3,32,32]{3,2,1,0:T(8,128)(2,1)S(1)} %copy-done.3), kind=kOutput, calls=%fused_computation.40 | convolution fusion | flops 67108864 | bytes 6299648 | tf_op jit(solution)/shard_map/ij,ojrw->oirw/dot_general | solution.py:50
  33.3 0.0 copy-start.2
  33.3 0.0 copy-start.4
  33.3 0.0 copy-start.5
  33.3 0.0 copy-start.6
  33.3 0.0 copy-start.7
  33.3 0.0 copy-start.8
  33.4 1.7 %collective-permute-done = bf16[1,32,4,8192]{3,1,2,0:T(8,128)(2,1)} collective-permute-done((bf16[1,32,4,8192]{3,1,2,0:T(8,128)(2,1)}, bf16[1,32,4,8192]{3,1,2,0:T(8,128)(2,1)}, u32[]{:S(2)}, u32[]{:S(2)}) %collective-permute-start) | collective-permute-done | bytes 2097184 | tf_op jit(solution)/shard_map/ppermute | solution.py:22
  35.0 2.3 %fusion.10 = bf16[4,8192,32]{1,2,0:T(8,128)(2,1)S(1)} fusion(f32[4,8192,32]{1,2,0:T(8,128)S(1)} %fusion.22, f32[4,8192,32]{1,2,0:T(8,128)S(1)} %fusion.25, bf16[1,32,4,8192]{3,1,2,0:T(8,128)(2,1)} %collective-permute-done, bf16[2,3,32,32]{3,2,1,0:T(8,128)(2,1)S(1)} %copy-done.3), kind=kOutput, calls=%fused_computation.18 | convolution fusion | flops 70254592 | bytes 12591104 | tf_op jit(solution)/shard_map/ij,ojrw->oirw/dot_general | solution.py:50
  37.3 1.0 fusion.95
  38.4 3.8 %collective-permute-start.2 = (bf16[1,32,1,8192]{3,1,2,0:T(8,128)(2,1)}, bf16[1,32,1,8192]{3,1,2,0:T(8,128)(2,1)S(1)}, u32[]{:S(2)}, u32[]{:S(2)}) collective-permute-start(bf16[1,32,1,8192]{3,1,2,0:T(8,128)(2,1)} %get-tuple-element.11), channel_id=1, source_target_pairs={{0,16},{16,32},{32,48},{48,64},{64,80},{80,96},{96,112},{112,128},... | collective-permute-start | bytes 1572872 | tf_op jit(solution)/shard_map/ppermute | solution.py:22
  42.2 6.1 %collective-permute-start.3 = (bf16[1,32,1,8192]{3,1,2,0:T(8,128)(2,1)}, bf16[1,32,1,8192]{3,1,2,0:T(8,128)(2,1)S(1)}, u32[]{:S(2)}, u32[]{:S(2)}) collective-permute-start(bf16[1,32,1,8192]{3,1,2,0:T(8,128)(2,1)} %get-tuple-element.12), channel_id=1, source_target_pairs={{16,0},{32,16},{48,32},{64,48},{80,64},{96,80},{112,96},{128,112},... | collective-permute-start | bytes 1572872 | tf_op jit(solution)/shard_map/ppermute | solution.py:25
  48.3 0.0 copy-done.2
  48.3 0.0 copy-done.4
  48.3 0.0 copy-done.5
  48.3 0.0 copy-done.6
  48.4 0.0 copy-done.7
  48.4 0.3 fusion.28
  48.7 0.1 slice.132
  48.8 0.1 slice.131
  49.0 0.1 slice.121
  49.1 0.0 copy-done.8
  49.1 6.6 %collective-permute-done.2 = bf16[1,32,1,8192]{3,1,2,0:T(8,128)(2,1)S(1)} collective-permute-done((bf16[1,32,1,8192]{3,1,2,0:T(8,128)(2,1)}, bf16[1,32,1,8192]{3,1,2,0:T(8,128)(2,1)S(1)}, u32[]{:S(2)}, u32[]{:S(2)}) %collective-permute-start.2) | collective-permute-done | bytes 524320 | tf_op jit(solution)/shard_map/ppermute | solution.py:22
  55.7 1.3 %collective-permute-done.3 = bf16[1,32,1,8192]{3,1,2,0:T(8,128)(2,1)S(1)} collective-permute-done((bf16[1,32,1,8192]{3,1,2,0:T(8,128)(2,1)}, bf16[1,32,1,8192]{3,1,2,0:T(8,128)(2,1)S(1)}, u32[]{:S(2)}, u32[]{:S(2)}) %collective-permute-start.3) | collective-permute-done | bytes 524320 | tf_op jit(solution)/shard_map/ppermute | solution.py:25
  57.0 0.4 fusion.18
  57.4 0.0 copy-start.1
  57.4 1.0 convolution_bitcast_fusion.5
  58.4 0.3 copy-done.1
  58.7 1.0 convolution_bitcast_fusion.3
  59.8 0.1 slice_bitcast_fusion.6
  59.8 1.5 %slice_bitcast_fusion.2 = (f32[32,4,8191]{2,0,1:T(8,128)S(1)}, f32[32,4,8191]{2,0,1:T(8,128)S(1)}) fusion(f32[1,32,4,8192]{3,1,2,0:T(8,128)S(1)} %convolution_bitcast_fusion.3, f32[1,32,4,8192]{3,1,2,0:T(8,128)S(1)} %convolution_bitcast_fusion.5), kind=kLoop, calls=%fused_computation.27 | loop fusion | bytes 16775168 | tf_op jit(solution)/shard_map/jit(_roll_static)/concatenate | solution.py:69
  61.3 4.0 %fusion.13 = bf16[32,4,8192]{2,0,1:T(8,128)(2,1)S(1)} fusion(f32[32,4,8191]{2,0,1:T(8,128)S(1)} %get-tuple-element.18, f32[32,4,1]{2,0,1:T(8,128)S(1)} %get-tuple-element.20, f32[32,4,1]{2,0,1:T(8,128)S(1)} %get-tuple-element.19, f32[32,4,8191]{2,0,1:T(8,128)S(1)} %get-tuple-element.17, f32[32]{0:T(128)S(1)} %get-tuple-element.16, ...), kind=kOutput, calls=%fused_computation.21 | convolution fusion | flops 227540992 | bytes 16783488 | tf_op jit(solution)/shard_map/otij,otjrw->oirw/dot_general | solution.py:68
  65.3 3.4 %collective-permute-start.5 = (bf16[1,32,4,8192]{3,1,2,0:T(8,128)(2,1)S(1)}, bf16[1,32,4,8192]{3,1,2,0:T(8,128)(2,1)S(1)}, u32[]{:S(2)}, u32[]{:S(2)}) collective-permute-start(bf16[1,32,4,8192]{3,1,2,0:T(8,128)(2,1)S(1)} %bitcast.212), channel_id=1, source_target_pairs={{1,0},{2,1},{3,2},{4,3},{5,4},{6,5},{7,6},{8,7},{9,8},{10,9},{11,1... | collective-permute-start | bytes 6291464 | tf_op jit(solution)/shard_map/ppermute | solution.py:25
  68.7 0.0 collective-permute-start.4
  68.7 0.7 fusion.49
  69.4 22.9 %collective-permute-done.5 = bf16[1,32,4,8192]{3,1,2,0:T(8,128)(2,1)S(1)} collective-permute-done((bf16[1,32,4,8192]{3,1,2,0:T(8,128)(2,1)S(1)}, bf16[1,32,4,8192]{3,1,2,0:T(8,128)(2,1)S(1)}, u32[]{:S(2)}, u32[]{:S(2)}) %collective-permute-start.5) | collective-permute-done | bytes 2097184 | tf_op jit(solution)/shard_map/ppermute | solution.py:25
  92.2 0.7 fusion.19
  92.9 3.3 %collective-permute-done.4 = bf16[1,32,4,8192]{3,1,2,0:T(8,128)(2,1)S(1)} collective-permute-done((bf16[1,32,4,8192]{3,1,2,0:T(8,128)(2,1)S(1)}, bf16[1,32,4,8192]{3,1,2,0:T(8,128)(2,1)S(1)}, u32[]{:S(2)}, u32[]{:S(2)}) %collective-permute-start.4) | collective-permute-done | bytes 2097184 | tf_op jit(solution)/shard_map/ppermute | solution.py:22
  96.2 0.9 fusion.11
  97.1 1.0 fusion.94
  98.2 1.9 %collective-permute-start.6 = (bf16[1,32,1,8192]{3,1,2,0:T(8,128)(2,1)}, bf16[1,32,1,8192]{3,1,2,0:T(8,128)(2,1)S(1)}, u32[]{:S(2)}, u32[]{:S(2)}) collective-permute-start(bf16[1,32,1,8192]{3,1,2,0:T(8,128)(2,1)} %get-tuple-element.7), channel_id=1, source_target_pairs={{0,16},{16,32},{32,48},{48,64},{64,80},{80,96},{96,112},{112,128},... | collective-permute-start | bytes 1572872 | tf_op jit(solution)/shard_map/ppermute | solution.py:22
  100.1 7.8 %collective-permute-start.7 = (bf16[1,32,1,8192]{3,1,2,0:T(8,128)(2,1)}, bf16[1,32,1,8192]{3,1,2,0:T(8,128)(2,1)S(1)}, u32[]{:S(2)}, u32[]{:S(2)}) collective-permute-start(bf16[1,32,1,8192]{3,1,2,0:T(8,128)(2,1)} %get-tuple-element.8), channel_id=1, source_target_pairs={{16,0},{32,16},{48,32},{64,48},{80,64},{96,80},{112,96},{128,112},... | collective-permute-start | bytes 1572872 | tf_op jit(solution)/shard_map/ppermute | solution.py:25
  107.8 0.3 fusion.27
  108.2 0.1 slice.146
  108.3 0.1 slice.145
  108.4 0.1 slice.119
  108.6 4.5 %collective-permute-done.6 = bf16[1,32,1,8192]{3,1,2,0:T(8,128)(2,1)S(1)} collective-permute-done((bf16[1,32,1,8192]{3,1,2,0:T(8,128)(2,1)}, bf16[1,32,1,8192]{3,1,2,0:T(8,128)(2,1)S(1)}, u32[]{:S(2)}, u32[]{:S(2)}) %collective-permute-start.6) | collective-permute-done | bytes 524320 | tf_op jit(solution)/shard_map/ppermute | solution.py:22
  113.0 1.6 %collective-permute-done.7 = bf16[1,32,1,8192]{3,1,2,0:T(8,128)(2,1)S(1)} collective-permute-done((bf16[1,32,1,8192]{3,1,2,0:T(8,128)(2,1)}, bf16[1,32,1,8192]{3,1,2,0:T(8,128)(2,1)S(1)}, u32[]{:S(2)}, u32[]{:S(2)}) %collective-permute-start.7) | collective-permute-done | bytes 524320 | tf_op jit(solution)/shard_map/ppermute | solution.py:25
  114.6 0.4 fusion.16
  115.0 1.1 convolution_bitcast_fusion.2
  116.1 0.1 slice_bitcast_fusion.5
  116.2 0.3 slice_bitcast_fusion.1
  116.5 1.1 convolution_bitcast_fusion
  117.6 1.1 slice_bitcast_fusion
  118.7 3.4 %fusion.14 = bf16[1,32,4,8192]{3,1,2,0:T(8,128)(2,1)S(1)} fusion(f32[32,4,8191]{2,0,1:T(8,128)S(1)} %slice_bitcast_fusion.1, f32[32,4,1]{2,0,1:T(8,128)S(1)} %slice_bitcast_fusion.5, f32[32,4,1]{2,0,1:T(8,128)S(1)} %slice_bitcast_fusion.4, f32[32,4,8191]{2,0,1:T(8,128)S(1)} %slice_bitcast_fusion, f32[32]{0:T(128)S(1)} %get-tuple-element.15, ...), kind=kOutput, calls=%fused_computation.22 | convolution fusion | flops 227540992 | bytes 16783488 | tf_op jit(solution)/shard_map/otij,otjrw->oirw/dot_general | solution.py:68
  122.1 2.9 %copy.51 = bf16[1,32,4,8192]{3,2,1,0:T(4,128)(2,1)} copy(bf16[1,32,4,8192]{3,1,2,0:T(8,128)(2,1)S(1)} %fusion.14) | data formatting | bytes 4194304 | tf_op jit(solution)/shard_map/convert_element_type | solution.py:71
  (4 shorter events, 0.0 us)
Async XLA Ops:
  0.0 7.1 %copy-start = (bf16[1,32,4,8192]{3,2,1,0:T(4,128)(2,1)S(1)}, bf16[1,32,4,8192]{3,2,1,0:T(4,128)(2,1)}, u32[]{:S(2)}) copy-start(bf16[1,32,4,8192]{3,2,1,0:T(4,128)(2,1)} %param.7) | copy-start | bytes 6291460
  0.0 7.1 %copy-start.3 = (bf16[2,3,32,32]{3,2,1,0:T(8,128)(2,1)S(1)}, bf16[2,3,32,32]{3,2,1,0:T(8,128)(2,1)}, u32[]{:S(2)}) copy-start(bf16[2,3,32,32]{3,2,1,0:T(8,128)(2,1)} %param.8) | copy-start | bytes 36868
  4.2 26.8 %collective-permute-start.1 = (bf16[1,32,4,8192]{3,1,2,0:T(8,128)(2,1)}, bf16[1,32,4,8192]{3,1,2,0:T(8,128)(2,1)}, u32[]{:S(2)}, u32[]{:S(2)}) collective-permute-start(bf16[1,32,4,8192]{3,1,2,0:T(8,128)(2,1)} %copy.32), channel_id=1, source_target_pairs={{1,0},{2,1},{3,2},{4,3},{5,4},{6,5},{7,6},{8,7},{9,8},{10,9},{11,1... | collective-permute-start | bytes 6291464 | tf_op jit(solution)/shard_map/ppermute | solution.py:25
  7.1 27.9 %collective-permute-start = (bf16[1,32,4,8192]{3,1,2,0:T(8,128)(2,1)}, bf16[1,32,4,8192]{3,1,2,0:T(8,128)(2,1)}, u32[]{:S(2)}, u32[]{:S(2)}) collective-permute-start(bf16[1,32,4,8192]{3,1,2,0:T(8,128)(2,1)} %copy.32), channel_id=1, source_target_pairs={{0,1},{1,2},{2,3},{3,4},{4,5},{5,6},{6,7},{7,8},{8,9},{9,10},{10,1... | collective-permute-start | bytes 6291464 | tf_op jit(solution)/shard_map/ppermute | solution.py:22
  33.3 15.0 %copy-start.2 = (bf16[2,9,32,32]{3,2,1,0:T(8,128)(2,1)S(1)}, bf16[2,9,32,32]{3,2,1,0:T(8,128)(2,1)}, u32[]{:S(2)}) copy-start(bf16[2,9,32,32]{3,2,1,0:T(8,128)(2,1)} %param.9) | copy-start | bytes 110596
  33.3 15.0 %copy-start.4 = (f32[9,9]{1,0:T(8,128)S(1)}, f32[9,9]{1,0:T(8,128)}, u32[]{:S(2)}) copy-start(f32[9,9]{1,0:T(8,128)} %constant.35.clone) | copy-start | bytes 976
  33.3 15.0 %copy-start.5 = (f32[9,9]{1,0:T(8,128)S(1)}, f32[9,9]{1,0:T(8,128)}, u32[]{:S(2)}) copy-start(f32[9,9]{1,0:T(8,128)} %constant.34.clone) | copy-start | bytes 976
  33.3 15.0 %copy-start.6 = (f32[9]{0:T(128)S(1)}, f32[9]{0:T(128)}, u32[]{:S(2)}) copy-start(f32[9]{0:T(128)} %constant.38) | copy-start | bytes 112
  33.3 15.0 %copy-start.7 = (f32[9]{0:T(128)S(1)}, f32[9]{0:T(128)}, u32[]{:S(2)}) copy-start(f32[9]{0:T(128)} %constant.37) | copy-start | bytes 112
  33.3 15.7 %copy-start.8 = (f32[2,32]{1,0:T(2,128)S(1)}, f32[2,32]{1,0:T(2,128)}, u32[]{:S(2)}) copy-start(f32[2,32]{1,0:T(2,128)} %param.10) | copy-start | bytes 772
  38.4 17.4 %collective-permute-start.2 = (bf16[1,32,1,8192]{3,1,2,0:T(8,128)(2,1)}, bf16[1,32,1,8192]{3,1,2,0:T(8,128)(2,1)S(1)}, u32[]{:S(2)}, u32[]{:S(2)}) collective-permute-start(bf16[1,32,1,8192]{3,1,2,0:T(8,128)(2,1)} %get-tuple-element.11), channel_id=1, source_target_pairs={{0,16},{16,32},{32,48},{48,64},{64,80},{80,96},{96,112},{112,128},... | collective-permute-start | bytes 1572872 | tf_op jit(solution)/shard_map/ppermute | solution.py:22
  42.2 14.8 %collective-permute-start.3 = (bf16[1,32,1,8192]{3,1,2,0:T(8,128)(2,1)}, bf16[1,32,1,8192]{3,1,2,0:T(8,128)(2,1)S(1)}, u32[]{:S(2)}, u32[]{:S(2)}) collective-permute-start(bf16[1,32,1,8192]{3,1,2,0:T(8,128)(2,1)} %get-tuple-element.12), channel_id=1, source_target_pairs={{16,0},{32,16},{48,32},{64,48},{80,64},{96,80},{112,96},{128,112},... | collective-permute-start | bytes 1572872 | tf_op jit(solution)/shard_map/ppermute | solution.py:25
  57.4 1.3 %copy-start.1 = (bf16[1,1,32,4,8192]{4,2,3,1,0:T(8,128)(2,1)}, bf16[1,1,32,4,8192]{4,2,3,1,0:T(8,128)(2,1)S(1)}, u32[]{:S(2)}) copy-start(bf16[1,1,32,4,8192]{4,2,3,1,0:T(8,128)(2,1)S(1)} %get-tuple-element.10) | copy-start | bytes 6291460
  65.3 26.9 %collective-permute-start.5 = (bf16[1,32,4,8192]{3,1,2,0:T(8,128)(2,1)S(1)}, bf16[1,32,4,8192]{3,1,2,0:T(8,128)(2,1)S(1)}, u32[]{:S(2)}, u32[]{:S(2)}) collective-permute-start(bf16[1,32,4,8192]{3,1,2,0:T(8,128)(2,1)S(1)} %bitcast.212), channel_id=1, source_target_pairs={{1,0},{2,1},{3,2},{4,3},{5,4},{6,5},{7,6},{8,7},{9,8},{10,9},{11,1... | collective-permute-start | bytes 6291464 | tf_op jit(solution)/shard_map/ppermute | solution.py:25
  68.7 27.6 %collective-permute-start.4 = (bf16[1,32,4,8192]{3,1,2,0:T(8,128)(2,1)S(1)}, bf16[1,32,4,8192]{3,1,2,0:T(8,128)(2,1)S(1)}, u32[]{:S(2)}, u32[]{:S(2)}) collective-permute-start(bf16[1,32,4,8192]{3,1,2,0:T(8,128)(2,1)S(1)} %bitcast.213), channel_id=1, source_target_pairs={{0,1},{1,2},{2,3},{3,4},{4,5},{5,6},{6,7},{7,8},{8,9},{9,10},{10,1... | collective-permute-start | bytes 6291464 | tf_op jit(solution)/shard_map/ppermute | solution.py:22
  98.2 14.9 %collective-permute-start.6 = (bf16[1,32,1,8192]{3,1,2,0:T(8,128)(2,1)}, bf16[1,32,1,8192]{3,1,2,0:T(8,128)(2,1)S(1)}, u32[]{:S(2)}, u32[]{:S(2)}) collective-permute-start(bf16[1,32,1,8192]{3,1,2,0:T(8,128)(2,1)} %get-tuple-element.7), channel_id=1, source_target_pairs={{0,16},{16,32},{32,48},{48,64},{64,80},{80,96},{96,112},{112,128},... | collective-permute-start | bytes 1572872 | tf_op jit(solution)/shard_map/ppermute | solution.py:22
  100.1 14.5 %collective-permute-start.7 = (bf16[1,32,1,8192]{3,1,2,0:T(8,128)(2,1)}, bf16[1,32,1,8192]{3,1,2,0:T(8,128)(2,1)S(1)}, u32[]{:S(2)}, u32[]{:S(2)}) collective-permute-start(bf16[1,32,1,8192]{3,1,2,0:T(8,128)(2,1)} %get-tuple-element.8), channel_id=1, source_target_pairs={{16,0},{32,16},{48,32},{64,48},{80,64},{96,80},{112,96},{128,112},... | collective-permute-start | bytes 1572872 | tf_op jit(solution)/shard_map/ppermute | solution.py:25
where the time goes:
time: 126 us; the launch traced here: 125 us
  waiting for transfers between devices  62.7 us (50%)
  starting transfers between devices  25.9 us (21%)
  matrix products  22.1 us (18%)
  local copies, waits for them, and re-layouts  13.4 us (11%)
    ppermute x4, waiting for transfers between devices, extended_2(): lax.ppermute(lax.slice_in_dim(block, 0, width, axis=dim), axis, backward)  46.6 us
    ppermute x4, starting transfers between devices, extended_2(): lax.ppermute(lax.slice_in_dim(block, 0, width, axis=dim), axis, backward)  20.1 us
    ppermute x4, waiting for transfers between devices, extended_2(): lax.ppermute(lax.slice_in_dim(block, block.shape[dim] - width, None, axis...  16.1 us
    dot_general x6, matrix products, conv_layer(): jnp.einsum('otij,otjrw->oirw', taps, row_stack, preferred_element_type=jn...  11.6 us
    dot_general x6, matrix products, mix_orients(): jnp.einsum('ij,ojrw->oirw', mixing[offset], extended[offset:offset + coun...  9.78 us
    ppermute x4, starting transfers between devices, extended_2(): lax.ppermute(lax.slice_in_dim(block, block.shape[dim] - width, None, axis...  5.73 us
    unnamed x19, local copies, waits for them, and re-layouts  4.53 us
    concatenate x6, local copies, waits for them, and re-layouts, conv_layer(): term = jnp.roll(term, -col_shift, axis=3)  3.08 us
  transfers between devices with their start and end apart: 8, of which 8 were waited for; matrix products, arithmetic and copies ran while one was open for 6% of the time, Pallas kernels for 0%

commit v1 on v0

v1 whole, which is shorter than its diff:
```python
import functools

import jax
import jax.numpy as jnp
from jax import lax
from jax.experimental import pallas as pl
from jax.experimental.pallas import tpu as pltpu
from jax.sharding import PartitionSpec as P

LAYERS = 2
C = 32
MESH = pl.DeviceIdType.MESH
CHUNKS = 16
LAG = 2
CYCLE_TAPS = (0, 1, 2, 5, 8, 7, 6, 3)
BF = jnp.bfloat16
F32 = jnp.float32


def iota(shape, dim):
    return lax.broadcasted_iota(jnp.int32, shape, dim)


def one_hot(cond):
    return jnp.where(cond, 1.0, 0.0).astype(BF)


def build_mix(a_ref, w_ref, layer, rows, natural):
    depth = rows * C
    lane, chan = iota((C, depth), 1), iota((C, depth), 0)
    for r in range(rows):
        place = chan * rows + r if natural else chan + r * C
        pick = one_hot(lane == place)
        for k in range(3):
            block = jnp.dot(w_ref[layer, k], pick, preferred_element_type=F32)
            a_ref[r * C : (r + 1) * C, k * depth : (k + 1) * depth] = block.astype(BF)


def build_conv(c_ref, kern_ref, cyc_ref, layer, rows, orient, natural):
    depth = (rows + 2) * C
    for p, tap in enumerate(CYCLE_TAPS):
        cyc_ref[p] = kern_ref[layer, tap].astype(F32)
    low = orient // 2
    high = (orient + 1) // 2
    lane, chan = iota((C, depth), 1), iota((C, depth), 0)
    for dx in range(3):
        for r in range(rows):
            total = jnp.zeros((C, depth), F32)
            for dy in range(3):
                tap = 3 * dy + dx
                if tap == 4:
                    rot = kern_ref[layer, 4]
                else:
                    p = CYCLE_TAPS.index(tap)
                    first = cyc_ref[(p + 16 - low) % 8]
                    second = cyc_ref[(p + 16 - high) % 8]
                    rot = (0.5 * first + 0.5 * second).astype(BF)
                source = r + dy - 1
                if source < 0:
                    base = rows * C
                elif source >= rows:
                    base = (rows + 1) * C
                else:
                    base = source * C
                pick = one_hot(lane == chan + base)
                total = total + jnp.dot(rot, pick, preferred_element_type=F32)
            c_ref[r * C : (r + 1) * C, dx * depth : (dx + 1) * depth] = total.astype(BF)
    if natural:
        out, src = iota((rows * C, rows * C), 0), iota((rows * C, rows * C), 1)
        order = one_hot(out == (src % C) * rows + src // C)
        c_ref[...] = jnp.dot(order, c_ref[...], preferred_element_type=F32).astype(BF)


def build_bias(b_ref, bias_ref, layer, rows, natural):
    row, chan = iota((rows * C, C), 0), iota((rows * C, C), 1)
    place = row // rows if natural else row % C
    spread = jnp.where(place == chan, bias_ref[layer : layer + 1, :], 0.0)
    column = jnp.sum(spread, axis=1, keepdims=True)
    b_ref[layer] = jnp.broadcast_to(column, (rows * C, 128))


def kernel(
    orients,
    lats,
    x_hbm,
    w_hbm,
    k_hbm,
    bias_hbm,
    out_ref,
    own,
    left0,
    right0,
    left1,
    right1,
    mixed0,
    mixed1,
    top0,
    top1,
    bottom0,
    bottom1,
    current1,
    result,
    w_ref,
    k_ref,
    bias_ref,
    cyc,
    a0,
    a1,
    c0,
    c1,
    b_ref,
    local_sem,
    left_send,
    left_recv,
    right_send,
    right_recv,
    up_send,
    up_recv,
    down_send,
    down_recv,
    out_sem,
):
    rows, width = x_hbm.shape[2], x_hbm.shape[3]
    n = CHUNKS
    size = width // n
    edge = 128
    depth = rows * C
    orient = lax.axis_index("orient")
    lat = lax.axis_index("lat")
    right = {"orient": lax.rem(orient + 1, orients)}
    left = {"orient": lax.rem(orient + orients - 1, orients)}
    above = {"lat": lat - 1}
    below = {"lat": lat + 1}
    has_above = lat > 0
    has_below = lat < lats - 1

    def lanes(chunk):
        return pl.ds(pl.multiple_of(chunk * size, size), size)

    def remote(src, dst, send, recv, device):
        return pltpu.make_async_remote_copy(
            src_ref=src, dst_ref=dst, send_sem=send, recv_sem=recv, device_id=device, device_id_type=MESH
        )

    barrier = pltpu.get_barrier_semaphore()
    pl.semaphore_signal(barrier, inc=1, device_id=left, device_id_type=MESH)
    pl.semaphore_signal(barrier, inc=1, device_id=right, device_id_type=MESH)

    @pl.when(has_above)
    def _():
        pl.semaphore_signal(barrier, inc=1, device_id=above, device_id_type=MESH)

    @pl.when(has_below)
    def _():
        pl.semaphore_signal(barrier, inc=1, device_id=below, device_id_type=MESH)

    local = [
        pltpu.make_async_copy(w_hbm, w_ref, local_sem.at[0]),
        pltpu.make_async_copy(k_hbm, k_ref, local_sem.at[1]),
        pltpu.make_async_copy(bias_hbm, bias_ref, local_sem.at[2]),
        pltpu.make_async_copy(x_hbm.at[0], own, local_sem.at[3]),
    ]
    for copy in local:
        copy.start()

    peers = 2 + jnp.where(has_above, 1, 0) + jnp.where(has_below, 1, 0)
    pl.semaphore_wait(barrier, peers)

    def orient_copies(layer, chunk):
        s = lanes(chunk)
        if layer == 0:
            src, to_left, to_right = x_hbm.at[0, :, :, s], right0.at[:, :, s], left0.at[:, :, s]
        else:
            src, to_left, to_right = current1.at[:, s], right1.at[:, s], left1.at[:, s]
        return (
            remote(src, to_left, left_send.at[layer, chunk], left_recv.at[layer, chunk], left),
            remote(src, to_right, right_send.at[layer, chunk], right_recv.at[layer, chunk], right),
        )

    def lat_copies(layer, chunk):
        s = lanes(chunk)
        mixed, top, bottom = ((mixed0, top0, bottom0), (mixed1, top1, bottom1))[layer]
        return (
            remote(mixed.at[0:C, s], bottom.at[:, s], up_send.at[layer, chunk], up_recv.at[layer, chunk], above),
            remote(
                mixed.at[depth - C : depth, s], top.at[:, s], down_send.at[layer, chunk], down_recv.at[layer, chunk], below
            ),
        )

    @pl.loop(0, n)
    def _(chunk):
        for copy in orient_copies(0, chunk):
            copy.start()

    @pl.when(jnp.logical_not(has_above))
    def _():
        top0[...] = jnp.zeros_like(top0)
        top1[...] = jnp.zeros_like(top1)

    @pl.when(jnp.logical_not(has_below))
    def _():
        bottom0[...] = jnp.zeros_like(bottom0)
        bottom1[...] = jnp.zeros_like(bottom1)

    for copy in local:
        copy.wait()
    build_mix(a0, w_ref, 0, rows, True)
    build_mix(a1, w_ref, 1, rows, False)
    build_conv(c0, k_ref, cyc, 0, rows, orient, False)
    build_conv(c1, k_ref, cyc, 1, rows, orient, True)
    build_bias(b_ref, bias_ref, 0, rows, False)
    build_bias(b_ref, bias_ref, 1, rows, True)

    def mix(layer, chunk):
        s = lanes(chunk)
        if layer == 0:
            parts = [ref[:, :, s].reshape(depth, size) for ref in (left0, own, right0)]
        else:
            parts = [ref[:, s] for ref in (left1, current1, right1)]
        weights, mixed = ((a0, mixed0), (a1, mixed1))[layer]
        total = jnp.dot(weights[...], jnp.concatenate(parts, axis=0), preferred_element_type=F32)
        mixed[:, s] = total.astype(BF)

    def conv(layer, chunk):
        mixed, top, bottom, weights = ((mixed0, top0, bottom0, c0), (mixed1, top1, bottom1, c1))[layer]
        before = pl.ds(pl.multiple_of(lax.rem(chunk * size + width - edge, width), edge), edge)
        after = pl.ds(pl.multiple_of(lax.rem(chunk * size + size, width), edge), edge)

        def part(s):
            return jnp.concatenate([mixed[:, s], top[:, s], bottom[:, s]], axis=0)

        middle = part(lanes(chunk))
        wide = jnp.concatenate([part(before), middle, part(after)], axis=1)
        whole = size + 2 * edge
        west = pltpu.roll(wide, 1, 1)[:, edge : edge + size]
        east = pltpu.roll(wide, whole - 1, 1)[:, edge : edge + size]
        total = jnp.dot(weights[...], jnp.concatenate([west, middle, east], axis=0), preferred_element_type=F32)
        bias = jnp.tile(b_ref[layer], (1, size // 128))
        return jnp.maximum(total + bias, 0.0).astype(BF)

    for layer in range(LAYERS):

        @pl.loop(0, n + 2 + LAG)
        def _(step, layer=layer):
            @pl.when(step < n)
            def _():
                chunk = lax.rem(step + layer, n)
                for copy in orient_copies(layer, chunk):
                    copy.wait_recv()
                mix(layer, chunk)
                up, down = lat_copies(layer, chunk)

                @pl.when(has_above)
                def _():
                    up.start()

                @pl.when(has_below)
                def _():
                    down.start()

            @pl.when(jnp.logical_and(step >= LAG, step < n + LAG))
            def _():
                chunk = lax.rem(step - LAG + layer, n)
                up, down = lat_copies(layer, chunk)

                @pl.when(has_below)
                def _():
                    up.wait_recv()

                @pl.when(has_above)
                def _():
                    down.wait_recv()

            @pl.when(step >= LAG + 2)
            def _():
                chunk = lax.rem(step - LAG - 1 + layer, n)
                values = conv(layer, chunk)
                s = lanes(chunk)
                if layer == 0:
                    current1[:, s] = values
                    for copy in orient_copies(1, chunk):
                        copy.start()
                else:
                    result[:, :, s] = values.reshape(C, rows, size)
                    pltpu.make_async_copy(result.at[:, :, s], out_ref.at[0, :, :, s], out_sem.at[chunk]).start()

    @pl.loop(0, n)
    def _(chunk):
        s = lanes(chunk)
        pltpu.make_async_copy(result.at[:, :, s], out_ref.at[0, :, :, s], out_sem.at[chunk]).wait()
        for layer in range(LAYERS):
            for copy in orient_copies(layer, chunk):
                copy.wait_send()
            up, down = lat_copies(layer, chunk)

            @pl.when(has_above)
            def _():
                up.wait_send()

            @pl.when(has_below)
            def _():
                down.wait_send()


def solution(mesh):
    orients, lats = mesh.shape["orient"], mesh.shape["lat"]

    def local(features, mix_weights, kernels, bias_terms):
        _, _, rows, width = features.shape
        depth = rows * C
        raw = pltpu.VMEM((C, rows, width), BF)
        flat = pltpu.VMEM((depth, width), BF)
        row = pltpu.VMEM((C, width), BF)
        sems = pltpu.SemaphoreType.DMA((LAYERS, CHUNKS))
        hbm = pl.BlockSpec(memory_space=pltpu.MemorySpace.HBM)
        return pl.pallas_call(
            functools.partial(kernel, orients, lats),
            out_shape=jax.ShapeDtypeStruct(features.shape, BF),
            in_specs=[hbm] * 4,
            out_specs=pl.BlockSpec(memory_space=pl.ANY),
            scratch_shapes=[raw, raw, raw, flat, flat, flat, flat, row, row, row, row, flat, raw]
            + [
                pltpu.VMEM(mix_weights.shape, BF),
                pltpu.VMEM(kernels.shape, BF),
                pltpu.VMEM(bias_terms.shape, F32),
                pltpu.VMEM((8, C, C), F32),
                pltpu.VMEM((depth, 3 * depth), BF),
                pltpu.VMEM((depth, 3 * depth), BF),
                pltpu.VMEM((depth, 3 * (rows + 2) * C), BF),
                pltpu.VMEM((depth, 3 * (rows + 2) * C), BF),
                pltpu.VMEM((LAYERS, depth, 128), F32),
                pltpu.SemaphoreType.DMA((4,)),
            ]
            + [sems] * 8
            + [pltpu.SemaphoreType.DMA((CHUNKS,))],
            compiler_params=pltpu.CompilerParams(
                collective_id=0, has_side_effects=True, vmem_limit_bytes=40 << 20
            ),
        )(features, mix_weights, kernels, bias_terms)

    return jax.shard_map(
        local,
        mesh=mesh,
        in_specs=(P("orient", None, "lat", None), P(), P(), P()),
        out_specs=P("orient", None, "lat", None),
        check_vma=False,
    )
```

time: 126 us -> 94.6 us (0.75)
  Pallas kernels: 0 us -> 89 us
  waiting for transfers between devices: 62.7 us -> 0 us
  starting transfers between devices: 25.9 us -> 0 us
  matrix products: 22.1 us -> 0 us
  local copies, waits for them, and re-layouts: 13.4 us -> 5.3 us
    pallas_call x0 -> x1, Pallas kernels: none -> 89 us  [local(): pl.pallas_call(functools.partial(kernel, orients, lats), out_shape=jax.Sh...]
    ppermute x8 -> x0, waiting for transfers between devices: 62.7 us -> none  [the longest x4 46.6 us: extended_2(): lax.ppermute(lax.slice_in_dim(block, 0, width, axis=dim), axis, backward)]
    ppermute x8 -> x0, starting transfers between devices: 25.9 us -> none  [the longest x4 20.1 us: extended_2(): lax.ppermute(lax.slice_in_dim(block, 0, width, axis=dim), axis, backward)]
    dot_general x14 -> x0, matrix products: 22.1 us -> none  [the longest x6 11.6 us: conv_layer(): jnp.einsum('otij,otjrw->oirw', taps, row_stack, preferred_element_type=jn...]
    concatenate x6 -> x0, local copies, waits for them, and re-layouts: 3.08 us -> none  [conv_layer(): term = jnp.roll(term, -col_shift, axis=3)]
    convert_element_type x1 -> x0, local copies, waits for them, and re-layouts: 2.94 us -> none  [conv_layer(): jax.nn.relu(running + bias_row[None, :, None, None]).astype(jnp.bfloat16)]
    slice x9 -> x0, local copies, waits for them, and re-layouts: 2.82 us -> none  [the longest x2 2.1 us: extended_2(): lax.slice_in_dim(block, block.shape[dim] - width, None, axis=dim)]
    unnamed x19 -> x9, local copies, waits for them, and re-layouts: 4.53 us -> 5.3 us
  transfers between devices with their start and end apart: 8 -> 0, of which waited for: 8 -> 0; matrix products, arithmetic and copies ran while one was open for 6% -> 0% of each run, Pallas kernels for 0% -> 0%
where the time goes in v1:
time: 94.6 us; the launch traced here: 94.4 us
  Pallas kernels  89 us (94%)
  local copies, waits for them, and re-layouts  5.3 us (6%)
    pallas_call x1, Pallas kernels, local(): pl.pallas_call(functools.partial(kernel, orients, lats), out_shape=jax.Sh...  89 us
    unnamed x9, local copies, waits for them, and re-layouts  5.3 us

profile of v1, /device:TPU:16, one launch (start us, length us, event | category | flops | bytes accessed | tf_op | source)
XLA Modules:
  0.0 94.4 jit_solution(14869515260430834804)
XLA Ops:
  0.0 0.0 copy-start
  0.0 1.6 %copy-done = bf16[1,32,4,8192]{3,2,1,0:T(4,128)(2,1)S(1)} copy-done((bf16[1,32,4,8192]{3,2,1,0:T(4,128)(2,1)S(1)}, bf16[1,32,4,8192]{3,2,1,0:T(4,128)(2,1)}, u32[]{:S(2)}) %copy-start) | copy-done | bytes 2097176
  1.6 0.0 copy-start.1
  1.6 0.9 copy-done.1
  2.5 0.0 copy-start.2
  2.5 0.8 copy-done.2
  3.3 0.0 copy-start.3
  3.3 0.7 copy-done.3
  4.0 89.0 %shard_map.46 = bf16[1,32,4,8192]{3,2,1,0:T(4,128)(2,1)S(1)} custom-call(bf16[1,32,4,8192]{3,2,1,0:T(4,128)(2,1)S(1)} %copy-done, bf16[2,3,32,32]{3,2,1,0:T(8,128)(2,1)S(1)} %copy-done.2, bf16[2,9,32,32]{3,2,1,0:T(8,128)(2,1)S(1)} %copy-done.1, f32[2,32]{1,0:T(2,128)S(1)} %copy-done.3), custom_call_target="tpu_custom_call" | custom-call | tf_op jit(solution)/shard_map/pallas_call | solution.py:316
  93.0 1.3 %copy.6 = bf16[1,32,4,8192]{3,2,1,0:T(4,128)(2,1)} copy(bf16[1,32,4,8192]{3,2,1,0:T(4,128)(2,1)S(1)} %shard_map.46) | data formatting | bytes 4194304
Async XLA Ops:
  0.0 1.6 %copy-start = (bf16[1,32,4,8192]{3,2,1,0:T(4,128)(2,1)S(1)}, bf16[1,32,4,8192]{3,2,1,0:T(4,128)(2,1)}, u32[]{:S(2)}) copy-start(bf16[1,32,4,8192]{3,2,1,0:T(4,128)(2,1)} %x_hbm.1) | copy-start | bytes 6291460
  1.6 0.9 copy-start.1
  2.5 0.8 copy-start.2
  3.3 0.7 copy-start.3

commit v2 on v1

--- a/solution.py
+++ b/solution.py
@@ -11,7 +11,7 @@
 C = 32
 MESH = pl.DeviceIdType.MESH
 CHUNKS = 16
-LAG = 2
+LAG = 4
 CYCLE_TAPS = (0, 1, 2, 5, 8, 7, 6, 3)
 BF = jnp.bfloat16
 F32 = jnp.float32
@@ -25,19 +25,34 @@
     return jnp.where(cond, 1.0, 0.0).astype(BF)
 
 
-def build_mix(a_ref, w_ref, layer, rows, natural):
+def places(rows):
+    order = [0, rows - 1] + list(range(1, rows - 1))
+    return [order.index(r) for r in range(rows)]
+
+
+def build_mix0(a_ref, w_ref, rows):
     depth = rows * C
     lane, chan = iota((C, depth), 1), iota((C, depth), 0)
-    for r in range(rows):
-        place = chan * rows + r if natural else chan + r * C
-        pick = one_hot(lane == place)
+    for r, at in enumerate(places(rows)):
+        pick = one_hot(lane == chan * rows + r)
         for k in range(3):
-            block = jnp.dot(w_ref[layer, k], pick, preferred_element_type=F32)
+            block = jnp.dot(w_ref[0, k], pick, preferred_element_type=F32)
+            a_ref[at * C : (at + 1) * C, k * depth : (k + 1) * depth] = block.astype(BF)
+
+
+def build_mix1(a_ref, w_ref):
+    depth = 2 * C
+    lane, chan = iota((C, depth), 1), iota((C, depth), 0)
+    for r in range(2):
+        pick = one_hot(lane == chan + r * C)
+        for k in range(3):
+            block = jnp.dot(w_ref[1, k], pick, preferred_element_type=F32)
             a_ref[r * C : (r + 1) * C, k * depth : (k + 1) * depth] = block.astype(BF)
 
 
 def build_conv(c_ref, kern_ref, cyc_ref, layer, rows, orient, natural):
     depth = (rows + 2) * C
+    at = places(rows)
     for p, tap in enumerate(CYCLE_TAPS):
         cyc_ref[p] = kern_ref[layer, tap].astype(F32)
     low = orient // 2
@@ -61,13 +76,15 @@
                 elif source >= rows:
                     base = (rows + 1) * C
                 else:
-                    base = source * C
+                    base = at[source] * C
                 pick = one_hot(lane == chan + base)
                 total = total + jnp.dot(rot, pick, preferred_element_type=F32)
-            c_ref[r * C : (r + 1) * C, dx * depth : (dx + 1) * depth] = total.astype(BF)
+            c_ref[at[r] * C : (at[r] + 1) * C, dx * depth : (dx + 1) * depth] = total.astype(BF)
     if natural:
         out, src = iota((rows * C, rows * C), 0), iota((rows * C, rows * C), 1)
-        order = one_hot(out == (src % C) * rows + src // C)
+        order = jnp.zeros((rows * C, rows * C), BF)
+        for r in range(rows):
+            order = order + one_hot((src // C == at[r]) & (out == (src % C) * rows + r))
         c_ref[...] = jnp.dot(order, c_ref[...], preferred_element_type=F32).astype(BF)
 
 
@@ -166,15 +183,18 @@
     peers = 2 + jnp.where(has_above, 1, 0) + jnp.where(has_below, 1, 0)
     pl.semaphore_wait(barrier, peers)
 
-    def orient_copies(layer, chunk):
+    half = 2 * C
+
+    def orient_copies(phase, chunk):
         s = lanes(chunk)
-        if layer == 0:
+        if phase == 0:
             src, to_left, to_right = x_hbm.at[0, :, :, s], right0.at[:, :, s], left0.at[:, :, s]
         else:
-            src, to_left, to_right = current1.at[:, s], right1.at[:, s], left1.at[:, s]
+            part = slice(0, half) if phase == 1 else slice(half, depth)
+            src, to_left, to_right = current1.at[part, s], right1.at[part, s], left1.at[part, s]
         return (
-            remote(src, to_left, left_send.at[layer, chunk], left_recv.at[layer, chunk], left),
-            remote(src, to_right, right_send.at[layer, chunk], right_recv.at[layer, chunk], right),
+            remote(src, to_left, left_send.at[phase, chunk], left_recv.at[phase, chunk], left),
+            remote(src, to_right, right_send.at[phase, chunk], right_recv.at[phase, chunk], right),
         )
 
     def lat_copies(layer, chunk):
@@ -183,7 +203,7 @@
         return (
             remote(mixed.at[0:C, s], bottom.at[:, s], up_send.at[layer, chunk], up_recv.at[layer, chunk], above),
             remote(
-                mixed.at[depth - C : depth, s], top.at[:, s], down_send.at[layer, chunk], down_recv.at[layer, chunk], below
+                mixed.at[C:half, s], top.at[:, s], down_send.at[layer, chunk], down_recv.at[layer, chunk], below
             ),
         )
 
@@ -204,22 +224,24 @@
 
     for copy in local:
         copy.wait()
-    build_mix(a0, w_ref, 0, rows, True)
-    build_mix(a1, w_ref, 1, rows, False)
+    build_mix0(a0, w_ref, rows)
+    build_mix1(a1, w_ref)
     build_conv(c0, k_ref, cyc, 0, rows, orient, False)
     build_conv(c1, k_ref, cyc, 1, rows, orient, True)
     build_bias(b_ref, bias_ref, 0, rows, False)
     build_bias(b_ref, bias_ref, 1, rows, True)
 
-    def mix(layer, chunk):
+    def mix(phase, chunk):
         s = lanes(chunk)
-        if layer == 0:
+        if phase == 0:
             parts = [ref[:, :, s].reshape(depth, size) for ref in (left0, own, right0)]
+            total = jnp.dot(a0[...], jnp.concatenate(parts, axis=0), preferred_element_type=F32)
+            mixed0[:, s] = total.astype(BF)
         else:
-            parts = [ref[:, s] for ref in (left1, current1, right1)]
-        weights, mixed = ((a0, mixed0), (a1, mixed1))[layer]
-        total = jnp.dot(weights[...], jnp.concatenate(parts, axis=0), preferred_element_type=F32)
-        mixed[:, s] = total.astype(BF)
+            part = slice(0, half) if phase == 1 else slice(half, depth)
+            parts = [ref[part, s] for ref in (left1, current1, right1)]
+            total = jnp.dot(a1[...], jnp.concatenate(parts, axis=0), preferred_element_type=F32)
+            mixed1[part, s] = total.astype(BF)
 
     def conv(layer, chunk):
         mixed, top, bottom, weights = ((mixed0, top0, bottom0, c0), (mixed1, top1, bottom1, c1))[layer]
@@ -238,59 +260,85 @@
         bias = jnp.tile(b_ref[layer], (1, size // 128))
         return jnp.maximum(total + bias, 0.0).astype(BF)
 
-    for layer in range(LAYERS):
-
-        @pl.loop(0, n + 2 + LAG)
-        def _(step, layer=layer):
-            @pl.when(step < n)
-            def _():
-                chunk = lax.rem(step + layer, n)
-                for copy in orient_copies(layer, chunk):
-                    copy.wait_recv()
-                mix(layer, chunk)
-                up, down = lat_copies(layer, chunk)
-
-                @pl.when(has_above)
-                def _():
-                    up.start()
-
-                @pl.when(has_below)
-                def _():
-                    down.start()
-
-            @pl.when(jnp.logical_and(step >= LAG, step < n + LAG))
-            def _():
-                chunk = lax.rem(step - LAG + layer, n)
-                up, down = lat_copies(layer, chunk)
-
-                @pl.when(has_below)
-                def _():
-                    up.wait_recv()
-
-                @pl.when(has_above)
-                def _():
-                    down.wait_recv()
-
-            @pl.when(step >= LAG + 2)
-            def _():
-                chunk = lax.rem(step - LAG - 1 + layer, n)
-                values = conv(layer, chunk)
-                s = lanes(chunk)
-                if layer == 0:
-                    current1[:, s] = values
-                    for copy in orient_copies(1, chunk):
-                        copy.start()
-                else:
-                    result[:, :, s] = values.reshape(C, rows, size)
-                    pltpu.make_async_copy(result.at[:, :, s], out_ref.at[0, :, :, s], out_sem.at[chunk]).start()
+    def take(phase, chunk):
+        for copy in orient_copies(phase, chunk):
+            copy.wait_recv()
+        mix(phase, chunk)
+
+    def send_rows(layer, chunk):
+        up, down = lat_copies(layer, chunk)
+
+        @pl.when(has_above)
+        def _():
+            up.start()
+
+        @pl.when(has_below)
+        def _():
+            down.start()
+
+    def take_rows(layer, chunk):
+        up, down = lat_copies(layer, chunk)
+
+        @pl.when(has_below)
+        def _():
+            up.wait_recv()
+
+        @pl.when(has_above)
+        def _():
+            down.wait_recv()
+
+    @pl.loop(0, n + 2 + LAG)
+    def _(step):
+        @pl.when(step < n)
+        def _():
+            take(0, step)
+            send_rows(0, step)
+
+        @pl.when(jnp.logical_and(step >= LAG, step < n + LAG))
+        def _():
+            take_rows(0, step - LAG)
+
+        @pl.when(step >= LAG + 2)
+        def _():
+            chunk = lax.rem(step - LAG - 1, n)
+            current1[:, lanes(chunk)] = conv(0, chunk)
+            for copy in orient_copies(1, chunk):
+                copy.start()
+
+    @pl.loop(0, n)
+    def _(step):
+        for copy in orient_copies(2, lax.rem(step + 1, n)):
+            copy.start()
+
+    @pl.loop(0, n)
+    def _(step):
+        chunk = lax.rem(step + 1, n)
+        take(1, chunk)
+        send_rows(1, chunk)
+
+    @pl.loop(0, n + 2)
+    def _(step):
+        @pl.when(step < n)
+        def _():
+            chunk = lax.rem(step + 1, n)
+            take_rows(1, chunk)
+            take(2, chunk)
+
+        @pl.when(step >= 2)
+        def _():
+            chunk = lax.rem(step, n)
+            s = lanes(chunk)
+            result[:, :, s] = conv(1, chunk).reshape(C, rows, size)
+            pltpu.make_async_copy(result.at[:, :, s], out_ref.at[0, :, :, s], out_sem.at[chunk]).start()
 
     @pl.loop(0, n)
     def _(chunk):
         s = lanes(chunk)
         pltpu.make_async_copy(result.at[:, :, s], out_ref.at[0, :, :, s], out_sem.at[chunk]).wait()
+        for phase in range(3):
+            for copy in orient_copies(phase, chunk):
+                copy.wait_send()
         for layer in range(LAYERS):
-            for copy in orient_copies(layer, chunk):
-                copy.wait_send()
             up, down = lat_copies(layer, chunk)
 
             @pl.when(has_above)
@@ -311,7 +359,8 @@
         raw = pltpu.VMEM((C, rows, width), BF)
         flat = pltpu.VMEM((depth, width), BF)
         row = pltpu.VMEM((C, width), BF)
-        sems = pltpu.SemaphoreType.DMA((LAYERS, CHUNKS))
+        sems = [pltpu.SemaphoreType.DMA((LAYERS, CHUNKS))] * 4
+        phase_sems = [pltpu.SemaphoreType.DMA((3, CHUNKS))] * 4
         hbm = pl.BlockSpec(memory_space=pltpu.MemorySpace.HBM)
         return pl.pallas_call(
             functools.partial(kernel, orients, lats),
@@ -325,18 +374,19 @@
                 pltpu.VMEM(bias_terms.shape, F32),
                 pltpu.VMEM((8, C, C), F32),
                 pltpu.VMEM((depth, 3 * depth), BF),
-                pltpu.VMEM((depth, 3 * depth), BF),
+                pltpu.VMEM((2 * C, 6 * C), BF),
                 pltpu.VMEM((depth, 3 * (rows + 2) * C), BF),
                 pltpu.VMEM((depth, 3 * (rows + 2) * C), BF),
                 pltpu.VMEM((LAYERS, depth, 128), F32),
                 pltpu.SemaphoreType.DMA((4,)),
             ]
-            + [sems] * 8
+            + phase_sems
+            + sems
             + [pltpu.SemaphoreType.DMA((CHUNKS,))],
             compiler_params=pltpu.CompilerParams(
                 collective_id=0, has_side_effects=True, vmem_limit_bytes=40 << 20
             ),
-        )(features, mix_weights, kernels, bias_terms)
+        )(*[pltpu.with_memory_space_constraint(v, pltpu.MemorySpace.HBM) for v in (features, mix_weights, kernels, bias_terms)])
 
     return jax.shard_map(
         local,

time: 94.6 us -> 78.9 us (0.83)
  the two profiles are of different devices: /device:TPU:16 before, /device:TPU:15 now
where the time goes in v2:
time: 78.9 us; the launch traced here: 78.8 us
  Pallas kernels  77.4 us (98%)
  local copies, waits for them, and re-layouts  1.32 us (2%)
    pallas_call x1, Pallas kernels, local(): pl.pallas_call(functools.partial(kernel, orients, lats), out_shape=jax.Sh...  77.4 us

profile of v2, /device:TPU:15, one launch (start us, length us, event | category | flops | bytes accessed | tf_op | source)
XLA Modules:
  0.0 78.8 jit_solution(9156565157533247223)
XLA Ops:
  0.0 77.4 %shard_map.46 = bf16[1,32,4,8192]{3,2,1,0:T(4,128)(2,1)S(1)} custom-call(bf16[1,32,4,8192]{3,2,1,0:T(4,128)(2,1)} %x_hbm.1, bf16[2,3,32,32]{3,2,1,0:T(8,128)(2,1)} %w_hbm.1, bf16[2,9,32,32]{3,2,1,0:T(8,128)(2,1)} %k_hbm.1, f32[2,32]{1,0:T(2,128)} %bias_hbm.1), custom_call_target="tpu_custom_call" | custom-call | tf_op jit(solution)/shard_map/pallas_call | solution.py:365
  77.5 1.3 %copy.6 = bf16[1,32,4,8192]{3,2,1,0:T(4,128)(2,1)} copy(bf16[1,32,4,8192]{3,2,1,0:T(4,128)(2,1)S(1)} %shard_map.46) | data formatting | bytes 4194304

commit v3 on v2

--- a/solution.py
+++ b/solution.py
@@ -11,7 +11,10 @@
 C = 32
 MESH = pl.DeviceIdType.MESH
 CHUNKS = 16
-LAG = 4
+LAG = 6
+RELAY_LAG = 3
+RELAY_LAG1 = 5
+ROUTES = 2
 CYCLE_TAPS = (0, 1, 2, 5, 8, 7, 6, 3)
 BF = jnp.bfloat16
 F32 = jnp.float32
@@ -135,6 +138,9 @@
     up_recv,
     down_send,
     down_recv,
+    relay,
+    relay_send,
+    relay_recv,
     out_sem,
 ):
     rows, width = x_hbm.shape[2], x_hbm.shape[3]
@@ -159,9 +165,26 @@
             src_ref=src, dst_ref=dst, send_sem=send, recv_sem=recv, device_id=device, device_id_type=MESH
         )
 
+    planes = lats // 2
+
+    place = lax.rem(orient // 2, orients // 4)
+    wrapped = jnp.logical_or(place == 0, place == orients // 4 - 1)
+    pairs = []
+    for turn in range(1, ROUTES):
+        pairs += [(planes - 1, planes + turn), (planes, planes - 1 - turn)]
+        if turn > 1:
+            pairs += [(planes, planes + turn), (planes - 1, planes - 1 - turn)]
+
     barrier = pltpu.get_barrier_semaphore()
-    pl.semaphore_signal(barrier, inc=1, device_id=left, device_id_type=MESH)
-    pl.semaphore_signal(barrier, inc=1, device_id=right, device_id_type=MESH)
+    peers = 2 + jnp.where(has_above, 1, 0) + jnp.where(has_below, 1, 0)
+    for one, two in pairs:
+        for here, there in ((one, two), (two, one)):
+            meets = jnp.logical_and(wrapped, lat == here)
+            peers = peers + jnp.where(meets, 1, 0)
+
+            @pl.when(meets)
+            def _(there=there):
+                pl.semaphore_signal(barrier, inc=1, device_id={"lat": there}, device_id_type=MESH)
 
     @pl.when(has_above)
     def _():
@@ -170,6 +193,9 @@
     @pl.when(has_below)
     def _():
         pl.semaphore_signal(barrier, inc=1, device_id=below, device_id_type=MESH)
+
+    pl.semaphore_signal(barrier, inc=1, device_id=left, device_id_type=MESH)
+    pl.semaphore_signal(barrier, inc=1, device_id=right, device_id_type=MESH)
 
     local = [
         pltpu.make_async_copy(w_hbm, w_ref, local_sem.at[0]),
@@ -180,7 +206,6 @@
     for copy in local:
         copy.start()
 
-    peers = 2 + jnp.where(has_above, 1, 0) + jnp.where(has_below, 1, 0)
     pl.semaphore_wait(barrier, peers)
 
     half = 2 * C
@@ -267,14 +292,65 @@
 
     def send_rows(layer, chunk):
         up, down = lat_copies(layer, chunk)
-
-        @pl.when(has_above)
+        s = lanes(chunk)
+        mixed = (mixed0, mixed1)[layer]
+        turn = jnp.where(wrapped, lax.rem(chunk, ROUTES), 0)
+        slot = chunk // ROUTES
+        via_down = jnp.logical_and(lat == planes - 1, turn != 0)
+        via_up = jnp.logical_and(lat == planes, turn != 0)
+
+        @pl.when(jnp.logical_and(has_above, jnp.logical_not(via_up)))
         def _():
             up.start()
 
-        @pl.when(has_below)
+        @pl.when(jnp.logical_and(has_below, jnp.logical_not(via_down)))
         def _():
             down.start()
+
+        @pl.when(via_up)
+        def _():
+            remote(
+                mixed.at[0:C, s],
+                relay.at[layer, slot],
+                up_send.at[layer, chunk],
+                relay_recv.at[layer, slot],
+                {"lat": planes - 1 - turn},
+            ).start()
+
+        @pl.when(via_down)
+        def _():
+            remote(
+                mixed.at[C:half, s],
+                relay.at[layer, slot],
+                down_send.at[layer, chunk],
+                relay_recv.at[layer, slot],
+                {"lat": planes + turn},
+            ).start()
+
+    def relay_copies(layer, chunk):
+        s = lanes(chunk)
+        top, bottom = ((top0, bottom0), (top1, bottom1))[layer]
+        slot = chunk // ROUTES
+        held, send, came = relay.at[layer, slot], relay_send.at[layer, slot], relay_recv.at[layer, slot]
+        return (
+            remote(held, held, send, came, {"lat": planes}),
+            remote(held, top.at[:, s], send, down_recv.at[layer, chunk], {"lat": planes}),
+            remote(held, bottom.at[:, s], send, up_recv.at[layer, chunk], {"lat": planes - 1}),
+        )
+
+    def pass_rows(layer, chunk):
+        turn = jnp.where(wrapped, lax.rem(chunk, ROUTES), 0)
+        arrival, onward_down, onward_up = relay_copies(layer, chunk)
+
+        @pl.when(jnp.logical_and(lat < planes - 1, turn == planes - 1 - lat))
+        def _():
+            arrival.wait_recv()
+            onward_up.start()
+
+        @pl.when(jnp.logical_and(lat > planes, turn == lat - planes))
+        def _():
+            arrival.wait_recv()
+            onward_down.start()
 
     def take_rows(layer, chunk):
         up, down = lat_copies(layer, chunk)
@@ -293,6 +369,10 @@
         def _():
             take(0, step)
             send_rows(0, step)
+
+        @pl.when(jnp.logical_and(step >= RELAY_LAG, step < n + RELAY_LAG))
+        def _():
+            pass_rows(0, step - RELAY_LAG)
 
         @pl.when(jnp.logical_and(step >= LAG, step < n + LAG))
         def _():
@@ -316,8 +396,16 @@
         take(1, chunk)
         send_rows(1, chunk)
 
+        @pl.when(step >= RELAY_LAG1)
+        def _():
+            pass_rows(1, lax.rem(step + 1 - RELAY_LAG1, n))
+
     @pl.loop(0, n + 2)
     def _(step):
+        @pl.when(step < RELAY_LAG1)
+        def _():
+            pass_rows(1, lax.rem(step + 1 + n - RELAY_LAG1, n))
+
         @pl.when(step < n)
         def _():
             chunk = lax.rem(step + 1, n)
@@ -349,6 +437,19 @@
             def _():
                 down.wait_send()
 
+    @pl.loop(0, n)
+    def _(chunk):
+        turn = jnp.where(wrapped, lax.rem(chunk, ROUTES), 0)
+        passed = jnp.logical_or(
+            jnp.logical_and(lat < planes - 1, turn == planes - 1 - lat),
+            jnp.logical_and(lat > planes, turn == lat - planes),
+        )
+
+        @pl.when(passed)
+        def _():
+            for layer in range(LAYERS):
+                relay_copies(layer, chunk)[0].wait_send()
+
 
 def solution(mesh):
     orients, lats = mesh.shape["orient"], mesh.shape["lat"]
@@ -360,6 +461,8 @@
         flat = pltpu.VMEM((depth, width), BF)
         row = pltpu.VMEM((C, width), BF)
         sems = [pltpu.SemaphoreType.DMA((LAYERS, CHUNKS))] * 4
+        slots = (CHUNKS + ROUTES - 1) // ROUTES
+        slot_sems = pltpu.SemaphoreType.DMA((LAYERS, slots))
         phase_sems = [pltpu.SemaphoreType.DMA((3, CHUNKS))] * 4
         hbm = pl.BlockSpec(memory_space=pltpu.MemorySpace.HBM)
         return pl.pallas_call(
@@ -382,6 +485,7 @@
             ]
             + phase_sems
             + sems
+            + [pltpu.VMEM((LAYERS, slots, C, width // CHUNKS), BF), slot_sems, slot_sems]
             + [pltpu.SemaphoreType.DMA((CHUNKS,))],
             compiler_params=pltpu.CompilerParams(
                 collective_id=0, has_side_effects=True, vmem_limit_bytes=40 << 20

time: 78.9 us -> 72.4 us (0.918)
  the two profiles are of different devices: /device:TPU:15 before, /device:TPU:16 now
where the time goes in v3:
time: 72.4 us; the launch traced here: 71.2 us
  Pallas kernels  69.9 us (97%)
  local copies, waits for them, and re-layouts  1.32 us (2%)
    pallas_call x1, Pallas kernels, local(): pl.pallas_call(functools.partial(kernel, orients, lats), out_shape=jax.Sh...  69.9 us

profile of v3, /device:TPU:16, one launch (start us, length us, event | category | flops | bytes accessed | tf_op | source)
XLA Modules:
  0.0 71.2 jit_solution(13231842650939680441)
XLA Ops:
  0.0 69.9 %shard_map.46 = bf16[1,32,4,8192]{3,2,1,0:T(4,128)(2,1)S(1)} custom-call(bf16[1,32,4,8192]{3,2,1,0:T(4,128)(2,1)} %x_hbm.1, bf16[2,3,32,32]{3,2,1,0:T(8,128)(2,1)} %w_hbm.1, bf16[2,9,32,32]{3,2,1,0:T(8,128)(2,1)} %k_hbm.1, f32[2,32]{1,0:T(2,128)} %bias_hbm.1), custom_call_target="tpu_custom_call" | custom-call | tf_op jit(solution)/shard_map/pallas_call | solution.py:468
  69.9 1.3 %copy.6 = bf16[1,32,4,8192]{3,2,1,0:T(4,128)(2,1)} copy(bf16[1,32,4,8192]{3,2,1,0:T(4,128)(2,1)S(1)} %shard_map.46) | data formatting | bytes 4194304

commit v4 on v3

--- a/solution.py
+++ b/solution.py
@@ -11,10 +11,10 @@
 C = 32
 MESH = pl.DeviceIdType.MESH
 CHUNKS = 16
-LAG = 6
-RELAY_LAG = 3
-RELAY_LAG1 = 5
-ROUTES = 2
+LAG = 10
+RELAY_LAG = 5
+RELAY_LAG1 = 8
+ROUTES = 3
 CYCLE_TAPS = (0, 1, 2, 5, 8, 7, 6, 3)
 BF = jnp.bfloat16
 F32 = jnp.float32

time: 72.4 us -> 70.6 us (0.975); the launches traced: 71.2 us -> 70.5 us
  Pallas kernels: 69.9 us -> 69.1 us
    pallas_call x1, Pallas kernels: 69.9 us -> 69.1 us  [local(): pl.pallas_call(functools.partial(kernel, orients, lats), out_shape=jax.Sh...]
where the time goes in v4:
time: 70.6 us; the launch traced here: 70.5 us
  Pallas kernels  69.1 us (98%)
  local copies, waits for them, and re-layouts  1.32 us (2%)
    pallas_call x1, Pallas kernels, local(): pl.pallas_call(functools.partial(kernel, orients, lats), out_shape=jax.Sh...  69.1 us

profile of v4, /device:TPU:16, one launch (start us, length us, event | category | flops | bytes accessed | tf_op | source)
XLA Modules:
  0.0 70.5 jit_solution(9458513032031803968)
XLA Ops:
  0.0 69.1 %shard_map.46 = bf16[1,32,4,8192]{3,2,1,0:T(4,128)(2,1)S(1)} custom-call(bf16[1,32,4,8192]{3,2,1,0:T(4,128)(2,1)} %x_hbm.1, bf16[2,3,32,32]{3,2,1,0:T(8,128)(2,1)} %w_hbm.1, bf16[2,9,32,32]{3,2,1,0:T(8,128)(2,1)} %k_hbm.1, f32[2,32]{1,0:T(2,128)} %bias_hbm.1), custom_call_target="tpu_custom_call" | custom-call | tf_op jit(solution)/shard_map/pallas_call | solution.py:468
  69.1 1.3 %copy.6 = bf16[1,32,4,8192]{3,2,1,0:T(4,128)(2,1)} copy(bf16[1,32,4,8192]{3,2,1,0:T(4,128)(2,1)S(1)} %shard_map.46) | data formatting | bytes 4194304

commit v5 on v4

--- a/solution.py
+++ b/solution.py
@@ -10,10 +10,10 @@
 LAYERS = 2
 C = 32
 MESH = pl.DeviceIdType.MESH
-CHUNKS = 16
-LAG = 10
-RELAY_LAG = 5
-RELAY_LAG1 = 8
+CHUNKS = 8
+LAG = 5
+RELAY_LAG = 3
+RELAY_LAG1 = 4
 ROUTES = 3
 CYCLE_TAPS = (0, 1, 2, 5, 8, 7, 6, 3)
 BF = jnp.bfloat16

time: 70.6 us -> 70.1 us (level)
  Pallas kernels: 69.1 us -> 68.3 us
    pallas_call x1, Pallas kernels: 69.1 us -> 68.3 us  [local(): pl.pallas_call(functools.partial(kernel, orients, lats), out_shape=jax.Sh...]
where the time goes in v5:
time: 70.1 us; the launch traced here: 69.7 us
  Pallas kernels  68.3 us (97%)
  local copies, waits for them, and re-layouts  1.32 us (2%)
    pallas_call x1, Pallas kernels, local(): pl.pallas_call(functools.partial(kernel, orients, lats), out_shape=jax.Sh...  68.3 us

profile of v5, /device:TPU:16, one launch (start us, length us, event | category | flops | bytes accessed | tf_op | source)
XLA Modules:
  0.0 69.7 jit_solution(14891449457147530177)
XLA Ops:
  0.0 68.3 %shard_map.46 = bf16[1,32,4,8192]{3,2,1,0:T(4,128)(2,1)S(1)} custom-call(bf16[1,32,4,8192]{3,2,1,0:T(4,128)(2,1)} %x_hbm.1, bf16[2,3,32,32]{3,2,1,0:T(8,128)(2,1)} %w_hbm.1, bf16[2,9,32,32]{3,2,1,0:T(8,128)(2,1)} %k_hbm.1, f32[2,32]{1,0:T(2,128)} %bias_hbm.1), custom_call_target="tpu_custom_call" | custom-call | tf_op jit(solution)/shard_map/pallas_call | solution.py:468
  68.4 1.3 %copy.6 = bf16[1,32,4,8192]{3,2,1,0:T(4,128)(2,1)} copy(bf16[1,32,4,8192]{3,2,1,0:T(4,128)(2,1)S(1)} %shard_map.46) | data formatting | bytes 4194304
